TPU v7x, 128 devices: a whole 4x4x4 slice. The times are simulated.
128 devices in a mesh: row: 8 (over x, core), col: 16 (over z, y).
Axes of the slice: x: 4, y: 4, z: 4, core: 2. Of those that a mesh axis runs over, the one named last changes fastest.
Arguments:
- surface_head: float32 [512, 4096], P('row', 'col'), may hold values from -6 to 6
- conduct_x: float32 [512, 4096], P('row', 'col'), may hold values from 0.01 to 0.1
- conduct_y: float32 [512, 4096], P('row', 'col'), may hold values from 0.01 to 0.1
- porosity: float32 [512, 4096], P('row', 'col'), may hold values from 0.45 to 1
- rainfall: float32 [512, 4096], P('row', 'col'), may hold values from 0.005 to 0.1
- pipe_head: float32 [32, 32768], P(None, ('row', 'col')), may hold values from -6 to 6
- pipe_class: int32 [32768], P(('row', 'col')), may hold values from 0 to 3
- pipe_up: int32 [32768], P(('row', 'col')), may hold values from 0 to 4095
- pipe_down: int32 [32768], P(('row', 'col')), may hold values from 0 to 4095
- pipe_matrices: float32 [4, 32, 32], replicated
- link_cell: int32 [128, 128, 64], P(('row', 'col')), may hold values from -1 to 16383, as said below
- link_node: int32 [128, 128, 64], P(None, ('row', 'col')), may hold values from -1 to 8191, as said below
- link_coef: float32 [128, 128, 64], P(None, ('row', 'col')), may hold values from 0.05 to 0.4
Outputs:
- surface_out: float32 [512, 4096], P('row', 'col')
- pipe_out: float32 [32, 32768], P(None, ('row', 'col'))
Inputs may be any that keep to these rules, and one draw needn't show every extreme that they name: `link_cell`: for each source tile and pipe owner the live slots come first; each is a cell of the source tile counted row by row; the other slots are -1. In every draw some tile sends 64 live slots to some owner. `link_node`: -1 exactly where link_cell is -1 at the same source tile, owner and slot; else a node of the owner's pipes, numbered node * 256 + pipe.
All inputs are finite; a program needn't handle non-finite values.
Results may differ from a plain program's by a relative error of at most 0.00015.
Values sent between devices are 32-bit elements; how exact they have to be, the bound alone decides.
No kernel may reach another device: no remote copies, remote signals or barrier semaphores. Data moves between devices by JAX's collectives and lax.ppermute only.
A program may use at most 64 MiB of HBM per device.

v0:
```python
import jax
import jax.numpy as jnp
from jax import lax
from jax.sharding import PartitionSpec as P

CLASSES = 4
SWEEPS = 4
STEPS = 3
boundary_gain = 0.5


def passed_along(block, axis, distance):
    devices = range(lax.axis_size(axis))
    route = [(i - distance, i) for i in devices if i - distance in devices]
    return lax.ppermute(block, axis, route)


def with_halo(block, sides, width):
    for axis, dim in sides:
        count = lax.axis_size(axis)
        forward = [(i, i + 1) for i in range(count - 1)]
        backward = [(target, source) for source, target in forward]
        low = lax.ppermute(
            lax.slice_in_dim(block, block.shape[dim] - width, None, axis=dim), axis, forward
        )
        high = lax.ppermute(lax.slice_in_dim(block, 0, width, axis=dim), axis, backward)
        block = jnp.concatenate([low, block, high], axis=dim)
    return block


def sweep_once(
    center, north, south, west, east, north_gain, south_gain, west_gain, east_gain, inverse, source
):
    change = (
        north_gain * (north - center)
        + south_gain * (south - center)
        + west_gain * (west - center)
        + east_gain * (east - center)
    )
    return center + change * inverse + source


def body(
    surface_head,
    conduct_x,
    conduct_y,
    porosity,
    rainfall,
    pipe_head,
    pipe_class,
    pipe_up,
    pipe_down,
    pipe_matrices,
    link_cell,
    link_node,
    link_coef,
):
    tile_rows, tile_cols = surface_head.shape
    inverse = 1.0 / porosity
    from_above = passed_along(conduct_x[-1:, :], "row", 1)
    north_gain = jnp.concatenate([from_above, conduct_x[:-1, :]], axis=0)
    from_left = passed_along(conduct_y[:, -1:], "col", 1)
    west_gain = jnp.concatenate([from_left, conduct_y[:, :-1]], axis=1)
    cell_index = link_cell[0]
    cell_live = cell_index >= 0
    cell_safe = jnp.where(cell_live, cell_index, 0)
    node_index = link_node[:, 0, :]
    node_live = node_index >= 0
    node_safe = jnp.where(node_live, node_index, 0)
    link_gain = link_coef[:, 0, :]
    inverse_flat = inverse.reshape(-1)
    surface = surface_head
    pipe_state = pipe_head
    for coupling_step in range(STEPS):
        for sweep_index in range(SWEEPS):
            padded = with_halo(surface, (("row", 0), ("col", 1)), 1)
            surface = sweep_once(
                surface,
                padded[:-2, 1:-1],
                padded[2:, 1:-1],
                padded[1:-1, :-2],
                padded[1:-1, 2:],
                north_gain,
                conduct_x,
                west_gain,
                conduct_y,
                inverse,
                rainfall,
            )
        surface_flat = surface.reshape(-1)
        sent_heads = jnp.where(cell_live, surface_flat[cell_safe], 0.0)
        pipe_flat = pipe_state.reshape(-1)
        pipe_at_slots = jnp.where(node_live, pipe_flat[node_safe], 0.0)
        arrived = lax.all_to_all(
            sent_heads, ("row", "col"), split_axis=0, concat_axis=0, tiled=True
        )
        manhole_flow = jnp.where(node_live, link_gain * (arrived - pipe_at_slots), 0.0)
        inflow = jnp.zeros_like(pipe_flat).at[node_safe].add(manhole_flow).reshape(pipe_state.shape)
        returned = lax.all_to_all(
            manhole_flow, ("row", "col"), split_axis=0, concat_axis=0, tiled=True
        )
        surface = (
            surface_flat.at[cell_safe]
            .add(-(returned * inverse_flat[cell_safe]))
            .reshape(tile_rows, tile_cols)
        )
        first_heads, last_heads = (
            lax.all_gather(pipe_state[0], "col", axis=0, tiled=True),
            lax.all_gather(pipe_state[-1], "col", axis=0, tiled=True),
        )
        balance = pipe_state + inflow
        balance = balance.at[0].add(boundary_gain * last_heads[pipe_up])
        balance = balance.at[-1].add(boundary_gain * first_heads[pipe_down])
        updated = jnp.zeros_like(pipe_state)
        for class_index in range(CLASSES):
            product = jnp.dot(
                pipe_matrices[class_index],
                balance,
                precision=lax.Precision.HIGHEST,
                preferred_element_type=jnp.float32,
            )
            updated = jnp.where(pipe_class[None, :] == class_index, product, updated)
        pipe_state = updated
    return (surface, pipe_state)


def solution(mesh):
    placed = (
        P("row", "col"),
        P("row", "col"),
        P("row", "col"),
        P("row", "col"),
        P("row", "col"),
        P(None, ("row", "col")),
        P(("row", "col")),
        P(("row", "col")),
        P(("row", "col")),
        P(),
        P(("row", "col"), None, None),
        P(None, ("row", "col"), None),
        P(None, ("row", "col"), None),
    )
    return jax.shard_map(
        body,
        mesh=mesh,
        in_specs=placed,
        out_specs=(P("row", "col"), P(None, ("row", "col"))),
        check_vma=False,
    )
```

profile of v0, /device:TPU:1, one launch (start us, length us, event | category | flops | bytes accessed | tf_op | source)
XLA Modules:
  0.0 1038.9 jit_solution(1538303368657251957)
XLA Ops:
  1.4 3.3 collective-permute-start.2
  4.7 3.1 collective-permute-start.1
  8.5 2.5 collective-permute-start
  11.9 3.2 collective-permute-start.3
  20.0 4.0 collective-permute-start.4
  25.2 3.3 collective-permute-start.7
  28.6 3.0 collective-permute-start.6
  33.7 4.6 collective-permute-start.8
  38.3 23.2 %all-gather = f32[1,4096]{1,0:T(1,128)S(1)} all-gather(f32[1,256]{1,0:T(1,128)S(1)} %get-tuple-element.133), channel_id=2, replica_groups=mesh['row'=8,'col'=16] {'col'}, dimensions={1}, use_global_device_ids=true | all-gather | bytes 17408 | tf_op jit(solution)/shard_map/all_gather | solution.py:109
  63.3 7.5 collective-permute-start.11
  70.8 4.7 collective-permute-start.10
  77.7 4.0 collective-permute-start.12
  82.9 1.9 collective-permute-start.15
  84.8 5.3 collective-permute-start.14
  92.2 4.6 collective-permute-start.16
  96.8 19.4 %all-gather.1 = f32[1,4096]{1,0:T(1,128)S(1)} all-gather(f32[1,256]{1,0:T(1,128)S(1)} %get-tuple-element.132), channel_id=3, replica_groups=mesh['row'=8,'col'=16] {'col'}, dimensions={1}, use_global_device_ids=true | all-gather | bytes 17408 | tf_op jit(solution)/shard_map/all_gather | solution.py:108
  118.2 45.5 %gather_fusion = f32[8192]{0:T(1024)S(1)} fusion(f32[16384]{0:T(1024)S(1)} %bitcast.123, s32[8192]{0:T(1024)S(1)} %broadcast_clamp_fusion.1), kind=kCustom, calls=%fused_computation | custom fusion | bytes 98304 | tf_op jit(solution)/shard_map/gather | solution.py:91
  164.5 12.9 %all-to-all-start = ((f32[128,1,64]{2,1,0:T(1,128)}), f32[128,1,64]{2,1,0:T(1,128)S(1)}, u32[]{:S(2)}, u32[]{:S(2)}) async-start(f32[128,1,64]{2,1,0:T(1,128)} %bitcast.2), calls=%async_computation | async-start | bytes 131072 | tf_op jit(solution)/shard_map/all_to_all | solution.py:94
  177.5 45.5 %gather_fusion.1 = f32[8192]{0:T(1024)S(1)} fusion(f32[8192]{0:T(1024)S(1)} %bitcast.130, s32[8192]{0:T(1024)S(1)} %broadcast_clamp_fusion), kind=kCustom, calls=%fused_computation.1 | custom fusion | bytes 98304 | tf_op jit(solution)/shard_map/gather | solution.py:93
  224.1 45.5 %gather_fusion.2 = f32[8192]{0:T(1024)S(1)} fusion(f32[16384]{0:T(1024)S(1)} %bitcast.132, s32[8192]{0:T(1024)S(1)} %broadcast_clamp_fusion.1), kind=kCustom, calls=%fused_computation.2 | custom fusion | bytes 98304 | tf_op jit(solution)/shard_map/gather | solution.py:104
  270.3 9.8 all-to-all-start.1
  280.2 44.9 %scatter_custom_fusion.1 = f32[8192]{0:T(1024)S(1)} fusion(s32[8192]{0:T(1024)S(1)} %reshape.369, f32[8192]{0:T(1024)S(1)} %reshape.475, f32[]{:T(128)} %constant.152.clone.1), kind=kCustom, calls=%fused_computation.362 | custom fusion | flops 8192 | bytes 32772 | tf_op jit(solution)/shard_map/scatter-add | solution.py:98
  325.3 50.3 %scatter_fusion = f32[16384]{0:T(1024)S(1)} fusion(f32[16384]{0:T(1024)S(1)} %bitcast.124, s32[8192]{0:T(1024)S(1)} %reshape.465, f32[8192]{0:T(1024)S(1)} %reshape.467), kind=kCustom, calls=%fused_computation.13 | custom fusion | flops 8192 | bytes 131072 | tf_op jit(solution)/shard_map/scatter-add | solution.py:104
  375.7 3.2 collective-permute-start.19
  378.9 2.4 collective-permute-start.18
  383.4 9.8 collective-permute-start.20
  394.4 1.9 collective-permute-start.23
  396.3 5.0 collective-permute-start.22
  403.4 4.6 collective-permute-start.24
  409.2 1.9 collective-permute-start.27
  411.1 5.0 collective-permute-start.26
  418.2 4.6 collective-permute-start.28
  422.8 25.7 %all-gather.2 = f32[1,4096]{1,0:T(1,128)S(1)} all-gather(f32[1,256]{1,0:T(1,128)S(1)} %get-tuple-element.131), channel_id=4, replica_groups=mesh['row'=8,'col'=16] {'col'}, dimensions={1}, use_global_device_ids=true | all-gather | bytes 17408 | tf_op jit(solution)/shard_map/all_gather | solution.py:109
  450.4 5.2 collective-permute-start.31
  455.6 7.0 collective-permute-start.30
  464.7 4.0 collective-permute-start.32
  468.7 17.2 %all-gather.3 = f32[1,4096]{1,0:T(1,128)S(1)} all-gather(f32[1,256]{1,0:T(1,128)S(1)} %get-tuple-element.130), channel_id=5, replica_groups=mesh['row'=8,'col'=16] {'col'}, dimensions={1}, use_global_device_ids=true | all-gather | bytes 17408 | tf_op jit(solution)/shard_map/all_gather | solution.py:108
  487.8 45.5 %gather_fusion.3 = f32[8192]{0:T(1024)S(1)} fusion(f32[16384]{0:T(1024)S(1)} %bitcast.125, s32[8192]{0:T(1024)S(1)} %broadcast_clamp_fusion.1), kind=kCustom, calls=%fused_computation.3 | custom fusion | bytes 98304 | tf_op jit(solution)/shard_map/gather | solution.py:91
  534.1 13.1 %all-to-all-start.2 = ((f32[128,1,64]{2,1,0:T(1,128)}), f32[128,1,64]{2,1,0:T(1,128)S(1)}, u32[]{:S(2)}, u32[]{:S(2)}) async-start(f32[128,1,64]{2,1,0:T(1,128)} %bitcast.9), calls=%async_computation.2 | async-start | bytes 131072 | tf_op jit(solution)/shard_map/all_to_all | solution.py:94
  547.2 45.5 %gather_fusion.6 = f32[8192]{0:T(1024)S(1)} fusion(f32[8192]{0:T(1024)S(1)} %bitcast.131, s32[8192]{0:T(1024)S(1)} %broadcast_clamp_fusion), kind=kCustom, calls=%fused_computation.6 | custom fusion | bytes 98304 | tf_op jit(solution)/shard_map/gather | solution.py:93
  593.5 9.8 all-to-all-start.3
  603.4 44.9 %scatter_custom_fusion.3 = f32[8192]{0:T(1024)S(1)} fusion(s32[8192]{0:T(1024)S(1)} %reshape.369, f32[8192]{0:T(1024)S(1)} %reshape.491, f32[]{:T(128)} %constant.152.clone.1), kind=kCustom, calls=%fused_computation.360 | custom fusion | flops 8192 | bytes 32772 | tf_op jit(solution)/shard_map/scatter-add | solution.py:98
  648.6 50.3 %scatter_fusion.1 = f32[16384]{0:T(1024)S(1)} fusion(f32[16384]{0:T(1024)S(1)} %bitcast.126, s32[8192]{0:T(1024)S(1)} %reshape.465, f32[8192]{0:T(1024)S(1)} %reshape.483), kind=kCustom, calls=%fused_computation.15 | custom fusion | flops 8192 | bytes 131072 | tf_op jit(solution)/shard_map/scatter-add | solution.py:104
  698.9 3.2 collective-permute-start.35
  702.1 2.4 collective-permute-start.34
  706.6 9.8 collective-permute-start.36
  717.6 1.9 collective-permute-start.39
  719.5 5.0 collective-permute-start.38
  726.6 4.6 collective-permute-start.40
  732.4 1.9 collective-permute-start.43
  734.3 5.0 collective-permute-start.42
  741.5 4.6 collective-permute-start.44
  746.0 25.7 %all-gather.4 = f32[1,4096]{1,0:T(1,128)S(1)} all-gather(f32[1,256]{1,0:T(1,128)S(1)} %get-tuple-element.129), channel_id=6, replica_groups=mesh['row'=8,'col'=16] {'col'}, dimensions={1}, use_global_device_ids=true | all-gather | bytes 17408 | tf_op jit(solution)/shard_map/all_gather | solution.py:109
  773.6 5.2 collective-permute-start.47
  778.8 7.0 collective-permute-start.46
  787.9 4.0 collective-permute-start.48
  791.9 17.2 %all-gather.5 = f32[1,4096]{1,0:T(1,128)S(1)} all-gather(f32[1,256]{1,0:T(1,128)S(1)} %get-tuple-element.128), channel_id=7, replica_groups=mesh['row'=8,'col'=16] {'col'}, dimensions={1}, use_global_device_ids=true | all-gather | bytes 17408 | tf_op jit(solution)/shard_map/all_gather | solution.py:108
  811.0 45.5 %gather_fusion.7 = f32[8192]{0:T(1024)S(1)} fusion(f32[16384]{0:T(1024)S(1)} %bitcast.127, s32[8192]{0:T(1024)S(1)} %broadcast_clamp_fusion.1), kind=kCustom, calls=%fused_computation.7 | custom fusion | bytes 98304 | tf_op jit(solution)/shard_map/gather | solution.py:91
  857.3 13.1 %all-to-all-start.4 = ((f32[128,1,64]{2,1,0:T(1,128)}), f32[128,1,64]{2,1,0:T(1,128)S(1)}, u32[]{:S(2)}, u32[]{:S(2)}) async-start(f32[128,1,64]{2,1,0:T(1,128)} %bitcast.27), calls=%async_computation.4 | async-start | bytes 131072 | tf_op jit(solution)/shard_map/all_to_all | solution.py:94
  870.4 45.5 %gather_fusion.10 = f32[8192]{0:T(1024)S(1)} fusion(f32[8192]{0:T(1024)S(1)} %bitcast.129, s32[8192]{0:T(1024)S(1)} %broadcast_clamp_fusion), kind=kCustom, calls=%fused_computation.10 | custom fusion | bytes 98304 | tf_op jit(solution)/shard_map/gather | solution.py:93
  916.2 44.9 %scatter_custom_fusion.5 = f32[8192]{0:T(1024)S(1)} fusion(s32[8192]{0:T(1024)S(1)} %reshape.369, f32[8192]{0:T(1024)S(1)} %reshape.507, f32[]{:T(128)} %constant.152.clone.1), kind=kCustom, calls=%fused_computation.358 | custom fusion | flops 8192 | bytes 32772 | tf_op jit(solution)/shard_map/scatter-add | solution.py:98
  962.4 15.8 %all-to-all-start.5 = ((f32[128,1,64]{2,1,0:T(1,128)}), f32[128,1,64]{2,1,0:T(1,128)S(1)}, u32[]{:S(2)}, u32[]{:S(2)}) async-start(f32[128,1,64]{2,1,0:T(1,128)} %bitcast.35), calls=%async_computation.5 | async-start | bytes 131072 | tf_op jit(solution)/shard_map/all_to_all | solution.py:99
  979.0 8.9 all-to-all-done.5
  988.0 50.3 %scatter_fusion.2 = f32[16384]{0:T(1024)S(1)} fusion(f32[16384]{0:T(1024)S(1)} %bitcast.128, s32[8192]{0:T(1024)S(1)} %reshape.465, f32[8192]{0:T(1024)S(1)} %reshape.499), kind=kCustom, calls=%fused_computation.17 | custom fusion | flops 8192 | bytes 131072 | tf_op jit(solution)/shard_map/scatter-add | solution.py:104
  (243 shorter events, 56.5 us)
Async XLA Ops:
  1.4 17.1 %collective-permute-start.2 = (f32[1,256]{1,0:T(1,128)S(1)}, f32[1,256]{1,0:T(1,128)S(1)}, u32[]{:S(2)}, u32[]{:S(2)}) collective-permute-start(f32[1,256]{1,0:T(1,128)S(1)} %get-tuple-element.127), channel_id=1, source_target_pairs={{16,0},{32,16},{48,32},{64,48},{80,64},{96,80},{112,96},{17,1},{33... | collective-permute-start | bytes 3080 | tf_op jit(solution)/shard_map/ppermute | solution.py:26
  4.7 13.8 %collective-permute-start.1 = (f32[1,256]{1,0:T(1,128)S(1)}, f32[1,256]{1,0:T(1,128)S(1)}, u32[]{:S(2)}, u32[]{:S(2)}) collective-permute-start(f32[1,256]{1,0:T(1,128)S(1)} %get-tuple-element.126), channel_id=1, source_target_pairs={{0,16},{16,32},{32,48},{48,64},{64,80},{80,96},{96,112},{1,17},{17... | collective-permute-start | bytes 3080 | tf_op jit(solution)/shard_map/ppermute | solution.py:23
  8.5 6.6 copy-start.7
  8.5 15.5 %collective-permute-start = (f32[1,256]{1,0:T(1,128)S(1)}, f32[1,256]{1,0:T(1,128)S(1)}, u32[]{:S(2)}, u32[]{:S(2)}) collective-permute-start(f32[1,256]{1,0:T(1,128)S(1)} %slice.500), channel_id=1, source_target_pairs={{0,16},{16,32},{32,48},{48,64},{64,80},{80,96},{96,112},{1,17},{17... | collective-permute-start | bytes 3080 | tf_op jit(solution)/shard_map/ppermute | solution.py:15
  11.9 12.2 %collective-permute-start.3 = (f32[64,1]{1,0:T(8,128)S(1)}, f32[64,1]{1,0:T(8,128)S(1)}, u32[]{:S(2)}, u32[]{:S(2)}) collective-permute-start(f32[64,1]{1,0:T(8,128)S(1)} %slice.506), channel_id=1, source_target_pairs={{0,1},{1,2},{2,3},{3,4},{4,5},{5,6},{6,7},{7,8},{8,9},{9,10},{10,1... | collective-permute-start | bytes 776 | tf_op jit(solution)/shard_map/ppermute | solution.py:15
  17.0 1.5 copy-start.5
  18.4 6.6 copy-start.3
  18.5 6.6 copy-start
  18.5 6.6 copy-start.1
  18.6 5.4 copy-start.11
  18.6 5.5 collective-permute-start.5
  20.0 5.0 collective-permute-start.4
  25.2 6.4 collective-permute-start.7
  28.6 3.7 collective-permute-start.6
  32.4 30.8 %collective-permute-start.9 = (f32[66,1]{1,0:T(8,128)S(1)}, f32[66,1]{1,0:T(8,128)S(1)}, u32[]{:S(2)}, u32[]{:S(2)}) collective-permute-start(f32[66,1]{1,0:T(8,128)S(1)} %get-tuple-element.101), channel_id=1, source_target_pairs={{1,0},{2,1},{3,2},{4,3},{5,4},{6,5},{7,6},{8,7},{9,8},{10,9},{11,1... | collective-permute-start | bytes 800 | tf_op jit(solution)/shard_map/ppermute | solution.py:26
  33.7 29.5 %collective-permute-start.8 = (f32[66,1]{1,0:T(8,128)S(1)}, f32[66,1]{1,0:T(8,128)S(1)}, u32[]{:S(2)}, u32[]{:S(2)}) collective-permute-start(f32[66,1]{1,0:T(8,128)S(1)} %get-tuple-element.100), channel_id=1, source_target_pairs={{0,1},{1,2},{2,3},{3,4},{4,5},{5,6},{6,7},{7,8},{8,9},{9,10},{10,1... | collective-permute-start | bytes 800 | tf_op jit(solution)/shard_map/ppermute | solution.py:23
  63.3 12.2 %collective-permute-start.11 = (f32[1,256]{1,0:T(1,128)S(1)}, f32[1,256]{1,0:T(1,128)S(1)}, u32[]{:S(2)}, u32[]{:S(2)}) collective-permute-start(f32[1,256]{1,0:T(1,128)S(1)} %get-tuple-element.123), channel_id=1, source_target_pairs={{16,0},{32,16},{48,32},{64,48},{80,64},{96,80},{112,96},{17,1},{33... | collective-permute-start | bytes 3080 | tf_op jit(solution)/shard_map/ppermute | solution.py:26
  70.8 5.4 collective-permute-start.10
  76.3 5.4 copy-start.12
  76.3 5.4 collective-permute-start.13
  77.7 5.0 collective-permute-start.12
  82.9 7.3 collective-permute-start.15
  84.8 6.0 collective-permute-start.14
  90.9 27.1 %collective-permute-start.17 = (f32[66,1]{1,0:T(8,128)S(1)}, f32[66,1]{1,0:T(8,128)S(1)}, u32[]{:S(2)}, u32[]{:S(2)}) collective-permute-start(f32[66,1]{1,0:T(8,128)S(1)} %get-tuple-element.97), channel_id=1, source_target_pairs={{1,0},{2,1},{3,2},{4,3},{5,4},{6,5},{7,6},{8,7},{9,8},{10,9},{11,1... | collective-permute-start | bytes 800 | tf_op jit(solution)/shard_map/ppermute | solution.py:26
  92.2 25.8 %collective-permute-start.16 = (f32[66,1]{1,0:T(8,128)S(1)}, f32[66,1]{1,0:T(8,128)S(1)}, u32[]{:S(2)}, u32[]{:S(2)}) collective-permute-start(f32[66,1]{1,0:T(8,128)S(1)} %get-tuple-element.96), channel_id=1, source_target_pairs={{0,1},{1,2},{2,3},{3,4},{4,5},{5,6},{6,7},{7,8},{8,9},{9,10},{10,1... | collective-permute-start | bytes 800 | tf_op jit(solution)/shard_map/ppermute | solution.py:23
  164.5 105.2 %all-to-all-start = ((f32[128,1,64]{2,1,0:T(1,128)}), f32[128,1,64]{2,1,0:T(1,128)S(1)}, u32[]{:S(2)}, u32[]{:S(2)}) async-start(f32[128,1,64]{2,1,0:T(1,128)} %bitcast.2), calls=%async_computation | async-start | bytes 131072 | tf_op jit(solution)/shard_map/all_to_all | solution.py:94
  270.3 54.9 %all-to-all-start.1 = ((f32[128,1,64]{2,1,0:T(1,128)}), f32[128,1,64]{2,1,0:T(1,128)S(1)}, u32[]{:S(2)}, u32[]{:S(2)}) async-start(f32[128,1,64]{2,1,0:T(1,128)} %bitcast.5), calls=%async_computation.1 | async-start | bytes 131072 | tf_op jit(solution)/shard_map/all_to_all | solution.py:99
  325.3 55.9 %copy-start.4 = (f32[4,32,32]{2,1,0:T(8,128)S(1)}, f32[4,32,32]{2,1,0:T(8,128)}, u32[]{:S(2)}) copy-start(f32[4,32,32]{2,1,0:T(8,128)} %param.34) | copy-start | bytes 49156
  375.7 5.8 collective-permute-start.19
  378.9 3.1 collective-permute-start.18
  382.1 11.3 %collective-permute-start.21 = (f32[66,1]{1,0:T(8,128)S(1)}, f32[66,1]{1,0:T(8,128)S(1)}, u32[]{:S(2)}, u32[]{:S(2)}) collective-permute-start(f32[66,1]{1,0:T(8,128)S(1)} %get-tuple-element.95), channel_id=1, source_target_pairs={{1,0},{2,1},{3,2},{4,3},{5,4},{6,5},{7,6},{8,7},{9,8},{10,9},{11,1... | collective-permute-start | bytes 800 | tf_op jit(solution)/shard_map/ppermute | solution.py:26
  383.4 10.9 %collective-permute-start.20 = (f32[66,1]{1,0:T(8,128)S(1)}, f32[66,1]{1,0:T(8,128)S(1)}, u32[]{:S(2)}, u32[]{:S(2)}) collective-permute-start(f32[66,1]{1,0:T(8,128)S(1)} %get-tuple-element.94), channel_id=1, source_target_pairs={{0,1},{1,2},{2,3},{3,4},{4,5},{5,6},{6,7},{7,8},{8,9},{9,10},{10,1... | collective-permute-start | bytes 800 | tf_op jit(solution)/shard_map/ppermute | solution.py:23
  394.4 7.1 collective-permute-start.23
  396.3 5.7 collective-permute-start.22
  402.1 6.1 collective-permute-start.25
  403.4 5.6 collective-permute-start.24
  409.2 7.0 collective-permute-start.27
  411.1 5.7 collective-permute-start.26
  416.9 33.3 %collective-permute-start.29 = (f32[66,1]{1,0:T(8,128)S(1)}, f32[66,1]{1,0:T(8,128)S(1)}, u32[]{:S(2)}, u32[]{:S(2)}) collective-permute-start(f32[66,1]{1,0:T(8,128)S(1)} %get-tuple-element.91), channel_id=1, source_target_pairs={{1,0},{2,1},{3,2},{4,3},{5,4},{6,5},{7,6},{8,7},{9,8},{10,9},{11,1... | collective-permute-start | bytes 800 | tf_op jit(solution)/shard_map/ppermute | solution.py:26
  418.2 32.0 %collective-permute-start.28 = (f32[66,1]{1,0:T(8,128)S(1)}, f32[66,1]{1,0:T(8,128)S(1)}, u32[]{:S(2)}, u32[]{:S(2)}) collective-permute-start(f32[66,1]{1,0:T(8,128)S(1)} %get-tuple-element.90), channel_id=1, source_target_pairs={{0,1},{1,2},{2,3},{3,4},{4,5},{5,6},{6,7},{7,8},{8,9},{9,10},{10,1... | collective-permute-start | bytes 800 | tf_op jit(solution)/shard_map/ppermute | solution.py:23
  450.4 12.2 %collective-permute-start.31 = (f32[1,256]{1,0:T(1,128)S(1)}, f32[1,256]{1,0:T(1,128)S(1)}, u32[]{:S(2)}, u32[]{:S(2)}) collective-permute-start(f32[1,256]{1,0:T(1,128)S(1)} %get-tuple-element.113), channel_id=1, source_target_pairs={{16,0},{32,16},{48,32},{64,48},{80,64},{96,80},{112,96},{17,1},{33... | collective-permute-start | bytes 3080 | tf_op jit(solution)/shard_map/ppermute | solution.py:26
  455.6 7.7 collective-permute-start.30
  463.4 24.2 %collective-permute-start.33 = (f32[66,1]{1,0:T(8,128)S(1)}, f32[66,1]{1,0:T(8,128)S(1)}, u32[]{:S(2)}, u32[]{:S(2)}) collective-permute-start(f32[66,1]{1,0:T(8,128)S(1)} %get-tuple-element.89), channel_id=1, source_target_pairs={{1,0},{2,1},{3,2},{4,3},{5,4},{6,5},{7,6},{8,7},{9,8},{10,9},{11,1... | collective-permute-start | bytes 800 | tf_op jit(solution)/shard_map/ppermute | solution.py:26
  464.7 22.9 %collective-permute-start.32 = (f32[66,1]{1,0:T(8,128)S(1)}, f32[66,1]{1,0:T(8,128)S(1)}, u32[]{:S(2)}, u32[]{:S(2)}) collective-permute-start(f32[66,1]{1,0:T(8,128)S(1)} %get-tuple-element.88), channel_id=1, source_target_pairs={{0,1},{1,2},{2,3},{3,4},{4,5},{5,6},{6,7},{7,8},{8,9},{9,10},{10,1... | collective-permute-start | bytes 800 | tf_op jit(solution)/shard_map/ppermute | solution.py:23
  534.1 58.8 %all-to-all-start.2 = ((f32[128,1,64]{2,1,0:T(1,128)}), f32[128,1,64]{2,1,0:T(1,128)S(1)}, u32[]{:S(2)}, u32[]{:S(2)}) async-start(f32[128,1,64]{2,1,0:T(1,128)} %bitcast.9), calls=%async_computation.2 | async-start | bytes 131072 | tf_op jit(solution)/shard_map/all_to_all | solution.py:94
  593.5 54.9 %all-to-all-start.3 = ((f32[128,1,64]{2,1,0:T(1,128)}), f32[128,1,64]{2,1,0:T(1,128)S(1)}, u32[]{:S(2)}, u32[]{:S(2)}) async-start(f32[128,1,64]{2,1,0:T(1,128)} %bitcast.23), calls=%async_computation.3 | async-start | bytes 131072 | tf_op jit(solution)/shard_map/all_to_all | solution.py:99
  698.9 5.8 collective-permute-start.35
  702.1 3.1 collective-permute-start.34
  705.3 11.3 %collective-permute-start.37 = (f32[66,1]{1,0:T(8,128)S(1)}, f32[66,1]{1,0:T(8,128)S(1)}, u32[]{:S(2)}, u32[]{:S(2)}) collective-permute-start(f32[66,1]{1,0:T(8,128)S(1)} %get-tuple-element.87), channel_id=1, source_target_pairs={{1,0},{2,1},{3,2},{4,3},{5,4},{6,5},{7,6},{8,7},{9,8},{10,9},{11,1... | collective-permute-start | bytes 800 | tf_op jit(solution)/shard_map/ppermute | solution.py:26
  706.6 10.9 %collective-permute-start.36 = (f32[66,1]{1,0:T(8,128)S(1)}, f32[66,1]{1,0:T(8,128)S(1)}, u32[]{:S(2)}, u32[]{:S(2)}) collective-permute-start(f32[66,1]{1,0:T(8,128)S(1)} %get-tuple-element.86), channel_id=1, source_target_pairs={{0,1},{1,2},{2,3},{3,4},{4,5},{5,6},{6,7},{7,8},{8,9},{9,10},{10,1... | collective-permute-start | bytes 800 | tf_op jit(solution)/shard_map/ppermute | solution.py:23
  717.6 7.1 collective-permute-start.39
  719.5 5.7 collective-permute-start.38
  725.3 6.1 collective-permute-start.41
  726.6 5.6 collective-permute-start.40
  732.4 7.0 collective-permute-start.43
  734.3 5.7 collective-permute-start.42
  740.2 33.3 %collective-permute-start.45 = (f32[66,1]{1,0:T(8,128)S(1)}, f32[66,1]{1,0:T(8,128)S(1)}, u32[]{:S(2)}, u32[]{:S(2)}) collective-permute-start(f32[66,1]{1,0:T(8,128)S(1)} %get-tuple-element.83), channel_id=1, source_target_pairs={{1,0},{2,1},{3,2},{4,3},{5,4},{6,5},{7,6},{8,7},{9,8},{10,9},{11,1... | collective-permute-start | bytes 800 | tf_op jit(solution)/shard_map/ppermute | solution.py:26
  741.5 32.0 %collective-permute-start.44 = (f32[66,1]{1,0:T(8,128)S(1)}, f32[66,1]{1,0:T(8,128)S(1)}, u32[]{:S(2)}, u32[]{:S(2)}) collective-permute-start(f32[66,1]{1,0:T(8,128)S(1)} %get-tuple-element.82), channel_id=1, source_target_pairs={{0,1},{1,2},{2,3},{3,4},{4,5},{5,6},{6,7},{7,8},{8,9},{9,10},{10,1... | collective-permute-start | bytes 800 | tf_op jit(solution)/shard_map/ppermute | solution.py:23
  773.6 12.2 %collective-permute-start.47 = (f32[1,256]{1,0:T(1,128)S(1)}, f32[1,256]{1,0:T(1,128)S(1)}, u32[]{:S(2)}, u32[]{:S(2)}) collective-permute-start(f32[1,256]{1,0:T(1,128)S(1)} %get-tuple-element.105), channel_id=1, source_target_pairs={{16,0},{32,16},{48,32},{64,48},{80,64},{96,80},{112,96},{17,1},{33... | collective-permute-start | bytes 3080 | tf_op jit(solution)/shard_map/ppermute | solution.py:26
  778.8 7.7 collective-permute-start.46
  786.6 24.2 %collective-permute-start.49 = (f32[66,1]{1,0:T(8,128)S(1)}, f32[66,1]{1,0:T(8,128)S(1)}, u32[]{:S(2)}, u32[]{:S(2)}) collective-permute-start(f32[66,1]{1,0:T(8,128)S(1)} %get-tuple-element.81), channel_id=1, source_target_pairs={{1,0},{2,1},{3,2},{4,3},{5,4},{6,5},{7,6},{8,7},{9,8},{10,9},{11,1... | collective-permute-start | bytes 800 | tf_op jit(solution)/shard_map/ppermute | solution.py:26
  787.9 22.9 %collective-permute-start.48 = (f32[66,1]{1,0:T(8,128)S(1)}, f32[66,1]{1,0:T(8,128)S(1)}, u32[]{:S(2)}, u32[]{:S(2)}) collective-permute-start(f32[66,1]{1,0:T(8,128)S(1)} %get-tuple-element.80), channel_id=1, source_target_pairs={{0,1},{1,2},{2,3},{3,4},{4,5},{5,6},{6,7},{7,8},{8,9},{9,10},{10,1... | collective-permute-start | bytes 800 | tf_op jit(solution)/shard_map/ppermute | solution.py:23
  857.3 58.8 %all-to-all-start.4 = ((f32[128,1,64]{2,1,0:T(1,128)}), f32[128,1,64]{2,1,0:T(1,128)S(1)}, u32[]{:S(2)}, u32[]{:S(2)}) async-start(f32[128,1,64]{2,1,0:T(1,128)} %bitcast.27), calls=%async_computation.4 | async-start | bytes 131072 | tf_op jit(solution)/shard_map/all_to_all | solution.py:94
  962.4 25.5 %all-to-all-start.5 = ((f32[128,1,64]{2,1,0:T(1,128)}), f32[128,1,64]{2,1,0:T(1,128)S(1)}, u32[]{:S(2)}, u32[]{:S(2)}) async-start(f32[128,1,64]{2,1,0:T(1,128)} %bitcast.35), calls=%async_computation.5 | async-start | bytes 131072 | tf_op jit(solution)/shard_map/all_to_all | solution.py:99
  (5 other events, 3.8 us)
where the time goes:
time: 1040 us
  local copies, waits for them, and re-layouts  339 us (33%)
  other arithmetic  291 us (28%)
  starting transfers between devices  254 us (24%)
  blocking collectives  128 us (12%)
  waiting for transfers between devices  21.3 us (2%)
    scatter-add x3, other arithmetic, body(): surface = surface_flat.at[cell_safe].add(-(returned * inverse_flat[cell_s...  151 us
    gather x9, local copies, waits for them, and re-layouts, body(): pipe_at_slots = jnp.where(node_live, pipe_flat[node_safe], 0.0)  137 us
    gather x6, local copies, waits for them, and re-layouts, body(): sent_heads = jnp.where(cell_live, surface_flat[cell_safe], 0.0)  137 us
    scatter-add x3, other arithmetic, body(): jnp.zeros_like(pipe_flat).at[node_safe].add(manhole_flow)  135 us
    ppermute x24, starting transfers between devices, with_halo(): lax.ppermute(lax.slice_in_dim(block, block.shape[dim] - width, None, axis...  118 us
    all_gather x3, blocking collectives, body(): lax.all_gather(pipe_state[-1], 'col', axis=0, tiled=True)  74.5 us
    ppermute x24, starting transfers between devices, with_halo(): lax.ppermute(lax.slice_in_dim(block, 0, width, axis=dim), axis, backward)  56 us
    all_gather x3, blocking collectives, body(): lax.all_gather(pipe_state[0], 'col', axis=0, tiled=True)  53.8 us
  transfers between devices with their start and end apart: 56, of which 18 were waited for; matrix products, arithmetic and copies ran while one was open for 28% of the time, Pallas kernels for 0%

commit v1 on v0

--- a/solution.py
+++ b/solution.py
@@ -1,3 +1,4 @@
+import functools
 import jax
 import jax.numpy as jnp
 from jax import lax
@@ -7,6 +8,16 @@
 SWEEPS = 4
 STEPS = 3
 boundary_gain = 0.5
+
+
+def remake_sites(t0, axis_name):
+    k_now = jax.lax.all_to_all(
+        jnp.concatenate(jax.lax.axis_size(axis_name) * [t0], 0), axis_name, 0, 0, tiled=True
+    )
+    return k_now
+
+
+detail_sheet = functools.partial(remake_sites, axis_name="col")
 
 
 def passed_along(block, axis, distance):
@@ -105,7 +116,7 @@
             .reshape(tile_rows, tile_cols)
         )
         first_heads, last_heads = (
-            lax.all_gather(pipe_state[0], "col", axis=0, tiled=True),
+            detail_sheet(pipe_state[0]),
             lax.all_gather(pipe_state[-1], "col", axis=0, tiled=True),
         )
         balance = pipe_state + inflow

time: 1040 us -> 1010 us (0.971)
  blocking collectives: 128 us -> 74.2 us
  waiting for transfers between devices: 21.3 us -> 48.3 us
    all_gather x3 -> x0, blocking collectives: 53.8 us -> none  [body(): lax.all_gather(pipe_state[0], 'col', axis=0, tiled=True)]
    all_to_all x3, waiting for transfers between devices: 0.01 us -> 27.4 us  [body(): lax.all_to_all(sent_heads, ('row', 'col'), split_axis=0, concat_axis=0, t...]
    all_to_all x3, starting transfers between devices: 35.3 us -> 18.4 us  [body(): lax.all_to_all(manhole_flow, ('row', 'col'), split_axis=0, concat_axis=0,...]
    all_to_all x0 -> x3, starting transfers between devices: none -> 15 us  [remake_sites(): jax.lax.all_to_all(jnp.concatenate(jax.lax.axis_size(axis_name) * [t0], 0...]
  transfers between devices with their start and end apart: 56 -> 59, of which waited for: 18 -> 20; matrix products, arithmetic and copies ran while one was open for 28% -> 34% of each run, Pallas kernels for 0% -> 0%
where the time goes in v1:
time: 1010 us; the launch traced here: 1000 us
  local copies, waits for them, and re-layouts  340 us (34%)
  other arithmetic  291 us (29%)
  starting transfers between devices  244 us (24%)
  blocking collectives  74.2 us (7%)
  waiting for transfers between devices  48.3 us (5%)
    scatter-add x3, other arithmetic, body(): surface = surface_flat.at[cell_safe].add(-(returned * inverse_flat[cell_s...  151 us
    gather x9, local copies, waits for them, and re-layouts, body(): pipe_at_slots = jnp.where(node_live, pipe_flat[node_safe], 0.0)  137 us
    gather x6, local copies, waits for them, and re-layouts, body(): sent_heads = jnp.where(cell_live, surface_flat[cell_safe], 0.0)  137 us
    scatter-add x3, other arithmetic, body(): jnp.zeros_like(pipe_flat).at[node_safe].add(manhole_flow)  135 us
    ppermute x24, starting transfers between devices, with_halo(): lax.ppermute(lax.slice_in_dim(block, block.shape[dim] - width, None, axis...  118 us
    all_gather x3, blocking collectives, body(): lax.all_gather(pipe_state[-1], 'col', axis=0, tiled=True)  74.2 us
    ppermute x24, starting transfers between devices, with_halo(): lax.ppermute(lax.slice_in_dim(block, 0, width, axis=dim), axis, backward)  56.2 us
    gather x2, local copies, waits for them, and re-layouts, body(): inverse_flat[cell_safe]  45.6 us
  transfers between devices with their start and end apart: 59, of which 20 were waited for; matrix products, arithmetic and copies ran while one was open for 34% of the time, Pallas kernels for 0%

profile of v1, /device:TPU:1, one launch (start us, length us, event | category | flops | bytes accessed | tf_op | source)
XLA Modules:
  0.0 1003.0 jit_solution(121059017126330213)
XLA Ops:
  1.4 3.3 collective-permute-start.2
  4.7 3.1 collective-permute-start.1
  8.5 2.5 collective-permute-start
  11.9 3.3 collective-permute-start.3
  15.8 7.5 all-to-all-start.3
  27.6 4.0 collective-permute-start.4
  32.8 3.6 collective-permute-start.7
  36.5 3.0 collective-permute-start.6
  41.6 4.6 collective-permute-start.8
  46.2 22.8 %all-gather = f32[1,4096]{1,0:T(1,128)S(1)} all-gather(f32[1,256]{1,0:T(1,128)S(1)} %get-tuple-element.133), channel_id=2, replica_groups=mesh['row'=8,'col'=16] {'col'}, dimensions={1}, use_global_device_ids=true | all-gather | bytes 17408 | tf_op jit(solution)/shard_map/all_gather | solution.py:120
  70.8 7.3 collective-permute-start.11
  78.2 4.7 collective-permute-start.10
  85.1 4.0 collective-permute-start.12
  90.3 1.9 collective-permute-start.15
  92.2 5.3 collective-permute-start.14
  97.8 45.5 %gather_fusion.1 = f32[8192]{0:T(1024)S(1)} fusion(f32[8192]{0:T(1024)S(1)} %bitcast.133, s32[8192]{0:T(1024)S(1)} %broadcast_clamp_fusion), kind=kCustom, calls=%fused_computation.1 | custom fusion | bytes 98304 | tf_op jit(solution)/shard_map/gather | solution.py:104
  145.7 4.6 collective-permute-start.16
  150.3 45.5 %gather_fusion.2 = f32[8192]{0:T(1024)S(1)} fusion(f32[16384]{0:T(1024)S(1)} %bitcast.135, s32[8192]{0:T(1024)S(1)} %broadcast_clamp_fusion.1), kind=kCustom, calls=%fused_computation.2 | custom fusion | bytes 98304 | tf_op jit(solution)/shard_map/gather | solution.py:115
  196.1 45.5 %gather_fusion = f32[8192]{0:T(1024)S(1)} fusion(f32[16384]{0:T(1024)S(1)} %bitcast.126, s32[8192]{0:T(1024)S(1)} %broadcast_clamp_fusion.1), kind=kCustom, calls=%fused_computation | custom fusion | bytes 98304 | tf_op jit(solution)/shard_map/gather | solution.py:102
  242.4 8.7 all-to-all-start
  252.8 8.0 all-to-all-done
  261.4 4.3 all-to-all-start.1
  265.8 44.9 %scatter_custom_fusion.1 = f32[8192]{0:T(1024)S(1)} fusion(s32[8192]{0:T(1024)S(1)} %reshape.483, f32[8192]{0:T(1024)S(1)} %reshape.589, f32[]{:T(128)} %constant.152.clone.1), kind=kCustom, calls=%fused_computation.362 | custom fusion | flops 8192 | bytes 32772 | tf_op jit(solution)/shard_map/scatter-add | solution.py:109
  311.0 50.3 %scatter_fusion = f32[16384]{0:T(1024)S(1)} fusion(f32[16384]{0:T(1024)S(1)} %bitcast.127, s32[8192]{0:T(1024)S(1)} %reshape.579, f32[8192]{0:T(1024)S(1)} %reshape.581), kind=kCustom, calls=%fused_computation.13 | custom fusion | flops 8192 | bytes 131072 | tf_op jit(solution)/shard_map/scatter-add | solution.py:115
  361.3 3.2 collective-permute-start.19
  364.5 2.4 collective-permute-start.18
  369.0 9.8 collective-permute-start.20
  380.0 1.9 collective-permute-start.23
  381.9 5.0 collective-permute-start.22
  389.0 4.6 collective-permute-start.24
  396.7 5.0 collective-permute-start.26
  403.8 4.6 collective-permute-start.28
  408.4 25.7 %all-gather.1 = f32[1,4096]{1,0:T(1,128)S(1)} all-gather(f32[1,256]{1,0:T(1,128)S(1)} %get-tuple-element.131), channel_id=3, replica_groups=mesh['row'=8,'col'=16] {'col'}, dimensions={1}, use_global_device_ids=true | all-gather | bytes 17408 | tf_op jit(solution)/shard_map/all_gather | solution.py:120
  436.0 5.2 collective-permute-start.31
  441.2 7.0 collective-permute-start.30
  448.2 45.5 %gather_fusion.6 = f32[8192]{0:T(1024)S(1)} fusion(f32[8192]{0:T(1024)S(1)} %bitcast.134, s32[8192]{0:T(1024)S(1)} %broadcast_clamp_fusion), kind=kCustom, calls=%fused_computation.6 | custom fusion | bytes 98304 | tf_op jit(solution)/shard_map/gather | solution.py:104
  494.5 3.8 all-to-all-start.6
  499.7 4.2 collective-permute-start.32
  506.6 45.5 %gather_fusion.3 = f32[8192]{0:T(1024)S(1)} fusion(f32[16384]{0:T(1024)S(1)} %bitcast.128, s32[8192]{0:T(1024)S(1)} %broadcast_clamp_fusion.1), kind=kCustom, calls=%fused_computation.3 | custom fusion | bytes 98304 | tf_op jit(solution)/shard_map/gather | solution.py:102
  552.9 10.8 %all-to-all-start.2 = ((f32[128,1,64]{2,1,0:T(1,128)}), f32[128,1,64]{2,1,0:T(1,128)S(1)}, u32[]{:S(2)}, u32[]{:S(2)}) async-start(f32[128,1,64]{2,1,0:T(1,128)} %bitcast.9), calls=%async_computation.2 | async-start | bytes 131072 | tf_op jit(solution)/shard_map/all_to_all | solution.py:105
  563.7 9.7 all-to-all-done.2
  574.1 4.3 all-to-all-start.4
  578.5 44.9 %scatter_custom_fusion.3 = f32[8192]{0:T(1024)S(1)} fusion(s32[8192]{0:T(1024)S(1)} %reshape.483, f32[8192]{0:T(1024)S(1)} %reshape.605, f32[]{:T(128)} %constant.152.clone.1), kind=kCustom, calls=%fused_computation.360 | custom fusion | flops 8192 | bytes 32772 | tf_op jit(solution)/shard_map/scatter-add | solution.py:109
  623.6 50.3 %scatter_fusion.1 = f32[16384]{0:T(1024)S(1)} fusion(f32[16384]{0:T(1024)S(1)} %bitcast.129, s32[8192]{0:T(1024)S(1)} %reshape.579, f32[8192]{0:T(1024)S(1)} %reshape.597), kind=kCustom, calls=%fused_computation.15 | custom fusion | flops 8192 | bytes 131072 | tf_op jit(solution)/shard_map/scatter-add | solution.py:115
  674.0 3.2 collective-permute-start.35
  677.2 2.4 collective-permute-start.34
  681.6 9.8 collective-permute-start.36
  694.6 5.0 collective-permute-start.38
  701.7 4.6 collective-permute-start.40
  709.4 5.0 collective-permute-start.42
  716.5 4.6 collective-permute-start.44
  721.1 25.7 %all-gather.2 = f32[1,4096]{1,0:T(1,128)S(1)} all-gather(f32[1,256]{1,0:T(1,128)S(1)} %get-tuple-element.129), channel_id=4, replica_groups=mesh['row'=8,'col'=16] {'col'}, dimensions={1}, use_global_device_ids=true | all-gather | bytes 17408 | tf_op jit(solution)/shard_map/all_gather | solution.py:120
  748.7 5.2 collective-permute-start.47
  753.9 7.0 collective-permute-start.46
  760.9 45.5 %gather_fusion.10 = f32[8192]{0:T(1024)S(1)} fusion(f32[8192]{0:T(1024)S(1)} %bitcast.132, s32[8192]{0:T(1024)S(1)} %broadcast_clamp_fusion), kind=kCustom, calls=%fused_computation.10 | custom fusion | bytes 98304 | tf_op jit(solution)/shard_map/gather | solution.py:104
  807.1 3.8 all-to-all-start.8
  812.3 4.0 collective-permute-start.48
  819.3 45.5 %gather_fusion.7 = f32[8192]{0:T(1024)S(1)} fusion(f32[16384]{0:T(1024)S(1)} %bitcast.130, s32[8192]{0:T(1024)S(1)} %broadcast_clamp_fusion.1), kind=kCustom, calls=%fused_computation.7 | custom fusion | bytes 98304 | tf_op jit(solution)/shard_map/gather | solution.py:102
  865.5 10.8 %all-to-all-start.5 = ((f32[128,1,64]{2,1,0:T(1,128)}), f32[128,1,64]{2,1,0:T(1,128)S(1)}, u32[]{:S(2)}, u32[]{:S(2)}) async-start(f32[128,1,64]{2,1,0:T(1,128)} %bitcast.28), calls=%async_computation.5 | async-start | bytes 131072 | tf_op jit(solution)/shard_map/all_to_all | solution.py:105
  876.4 9.7 all-to-all-done.5
  886.2 44.9 %scatter_custom_fusion.5 = f32[8192]{0:T(1024)S(1)} fusion(s32[8192]{0:T(1024)S(1)} %reshape.483, f32[8192]{0:T(1024)S(1)} %reshape.621, f32[]{:T(128)} %constant.152.clone.1), kind=kCustom, calls=%fused_computation.358 | custom fusion | flops 8192 | bytes 32772 | tf_op jit(solution)/shard_map/scatter-add | solution.py:109
  932.4 9.8 all-to-all-start.7
  943.0 8.9 all-to-all-done.7
  952.0 50.3 %scatter_fusion.2 = f32[16384]{0:T(1024)S(1)} fusion(f32[16384]{0:T(1024)S(1)} %bitcast.131, s32[8192]{0:T(1024)S(1)} %reshape.579, f32[8192]{0:T(1024)S(1)} %reshape.613), kind=kCustom, calls=%fused_computation.17 | custom fusion | flops 8192 | bytes 131072 | tf_op jit(solution)/shard_map/scatter-add | solution.py:115
  (249 shorter events, 63.2 us)
Async XLA Ops:
  1.4 24.6 %collective-permute-start.2 = (f32[1,256]{1,0:T(1,128)S(1)}, f32[1,256]{1,0:T(1,128)S(1)}, u32[]{:S(2)}, u32[]{:S(2)}) collective-permute-start(f32[1,256]{1,0:T(1,128)S(1)} %get-tuple-element.127), channel_id=1, source_target_pairs={{16,0},{32,16},{48,32},{64,48},{80,64},{96,80},{112,96},{17,1},{33... | collective-permute-start | bytes 3080 | tf_op jit(solution)/shard_map/ppermute | solution.py:37
  4.7 21.3 %collective-permute-start.1 = (f32[1,256]{1,0:T(1,128)S(1)}, f32[1,256]{1,0:T(1,128)S(1)}, u32[]{:S(2)}, u32[]{:S(2)}) collective-permute-start(f32[1,256]{1,0:T(1,128)S(1)} %get-tuple-element.126), channel_id=1, source_target_pairs={{0,16},{16,32},{32,48},{48,64},{64,80},{80,96},{96,112},{1,17},{17... | collective-permute-start | bytes 3080 | tf_op jit(solution)/shard_map/ppermute | solution.py:34
  8.5 6.7 copy-start.6
  8.5 23.2 %collective-permute-start = (f32[1,256]{1,0:T(1,128)S(1)}, f32[1,256]{1,0:T(1,128)S(1)}, u32[]{:S(2)}, u32[]{:S(2)}) collective-permute-start(f32[1,256]{1,0:T(1,128)S(1)} %slice.500), channel_id=1, source_target_pairs={{0,16},{16,32},{32,48},{48,64},{64,80},{80,96},{96,112},{1,17},{17... | collective-permute-start | bytes 3080 | tf_op jit(solution)/shard_map/ppermute | solution.py:26
  11.9 11.5 %copy-start.7 = (s32[1,128,64]{1,2,0:T(8,128)S(1)}, s32[1,128,64]{1,2,0:T(8,128)}, u32[]{:S(2)}) copy-start(s32[1,128,64]{1,2,0:T(8,128)} %param.35) | copy-start | bytes 98308
  11.9 19.8 %collective-permute-start.3 = (f32[64,1]{1,0:T(8,128)S(1)}, f32[64,1]{1,0:T(8,128)S(1)}, u32[]{:S(2)}, u32[]{:S(2)}) collective-permute-start(f32[64,1]{1,0:T(8,128)S(1)} %slice.506), channel_id=1, source_target_pairs={{0,1},{1,2},{2,3},{3,4},{4,5},{5,6},{6,7},{7,8},{8,9},{9,10},{10,1... | collective-permute-start | bytes 776 | tf_op jit(solution)/shard_map/ppermute | solution.py:26
  15.8 226.5 %all-to-all-start.3 = ((f32[16,256,1]{1,2,0:T(1,128)}), f32[16,256,1]{1,2,0:T(1,128)S(1)}, u32[]{:S(2)}, u32[]{:S(2)}) async-start(f32[16,256,1]{1,2,0:T(1,128)} %concatenate.271), calls=%async_computation.3 | async-start | bytes 32768 | tf_op jit(solution)/shard_map/all_to_all | solution.py:14
  26.1 6.6 copy-start.3
  26.1 6.6 copy-start
  26.2 5.5 collective-permute-start.5
  27.6 5.0 collective-permute-start.4
  32.8 6.7 collective-permute-start.7
  36.5 3.7 collective-permute-start.6
  40.3 30.4 %collective-permute-start.9 = (f32[66,1]{1,0:T(8,128)S(1)}, f32[66,1]{1,0:T(8,128)S(1)}, u32[]{:S(2)}, u32[]{:S(2)}) collective-permute-start(f32[66,1]{1,0:T(8,128)S(1)} %get-tuple-element.101), channel_id=1, source_target_pairs={{1,0},{2,1},{3,2},{4,3},{5,4},{6,5},{7,6},{8,7},{9,8},{10,9},{11,1... | collective-permute-start | bytes 800 | tf_op jit(solution)/shard_map/ppermute | solution.py:37
  41.6 29.1 %collective-permute-start.8 = (f32[66,1]{1,0:T(8,128)S(1)}, f32[66,1]{1,0:T(8,128)S(1)}, u32[]{:S(2)}, u32[]{:S(2)}) collective-permute-start(f32[66,1]{1,0:T(8,128)S(1)} %get-tuple-element.100), channel_id=1, source_target_pairs={{0,1},{1,2},{2,3},{3,4},{4,5},{5,6},{6,7},{7,8},{8,9},{9,10},{10,1... | collective-permute-start | bytes 800 | tf_op jit(solution)/shard_map/ppermute | solution.py:34
  70.8 12.1 %collective-permute-start.11 = (f32[1,256]{1,0:T(1,128)S(1)}, f32[1,256]{1,0:T(1,128)S(1)}, u32[]{:S(2)}, u32[]{:S(2)}) collective-permute-start(f32[1,256]{1,0:T(1,128)S(1)} %get-tuple-element.123), channel_id=1, source_target_pairs={{16,0},{32,16},{48,32},{64,48},{80,64},{96,80},{112,96},{17,1},{33... | collective-permute-start | bytes 3080 | tf_op jit(solution)/shard_map/ppermute | solution.py:37
  78.2 5.4 collective-permute-start.10
  83.7 5.4 collective-permute-start.13
  85.1 5.0 collective-permute-start.12
  90.3 54.0 %collective-permute-start.15 = (f32[1,256]{1,0:T(1,128)S(1)}, f32[1,256]{1,0:T(1,128)S(1)}, u32[]{:S(2)}, u32[]{:S(2)}) collective-permute-start(f32[1,256]{1,0:T(1,128)S(1)} %get-tuple-element.121), channel_id=1, source_target_pairs={{16,0},{32,16},{48,32},{64,48},{80,64},{96,80},{112,96},{17,1},{33... | collective-permute-start | bytes 3080 | tf_op jit(solution)/shard_map/ppermute | solution.py:37
  92.2 52.0 %collective-permute-start.14 = (f32[1,256]{1,0:T(1,128)S(1)}, f32[1,256]{1,0:T(1,128)S(1)}, u32[]{:S(2)}, u32[]{:S(2)}) collective-permute-start(f32[1,256]{1,0:T(1,128)S(1)} %get-tuple-element.120), channel_id=1, source_target_pairs={{0,16},{16,32},{32,48},{48,64},{64,80},{80,96},{96,112},{1,17},{17... | collective-permute-start | bytes 3080 | tf_op jit(solution)/shard_map/ppermute | solution.py:34
  144.4 51.5 %collective-permute-start.17 = (f32[66,1]{1,0:T(8,128)S(1)}, f32[66,1]{1,0:T(8,128)S(1)}, u32[]{:S(2)}, u32[]{:S(2)}) collective-permute-start(f32[66,1]{1,0:T(8,128)S(1)} %get-tuple-element.97), channel_id=1, source_target_pairs={{1,0},{2,1},{3,2},{4,3},{5,4},{6,5},{7,6},{8,7},{9,8},{10,9},{11,1... | collective-permute-start | bytes 800 | tf_op jit(solution)/shard_map/ppermute | solution.py:37
  145.7 50.3 %collective-permute-start.16 = (f32[66,1]{1,0:T(8,128)S(1)}, f32[66,1]{1,0:T(8,128)S(1)}, u32[]{:S(2)}, u32[]{:S(2)}) collective-permute-start(f32[66,1]{1,0:T(8,128)S(1)} %get-tuple-element.96), channel_id=1, source_target_pairs={{0,1},{1,2},{2,3},{3,4},{4,5},{5,6},{6,7},{7,8},{8,9},{9,10},{10,1... | collective-permute-start | bytes 800 | tf_op jit(solution)/shard_map/ppermute | solution.py:34
  242.4 18.4 %all-to-all-start = ((f32[128,1,64]{2,1,0:T(1,128)}), f32[128,1,64]{2,1,0:T(1,128)S(1)}, u32[]{:S(2)}, u32[]{:S(2)}) async-start(f32[128,1,64]{2,1,0:T(1,128)} %bitcast.2), calls=%async_computation | async-start | bytes 131072 | tf_op jit(solution)/shard_map/all_to_all | solution.py:105
  261.4 49.4 %all-to-all-start.1 = ((f32[128,1,64]{2,1,0:T(1,128)}), f32[128,1,64]{2,1,0:T(1,128)S(1)}, u32[]{:S(2)}, u32[]{:S(2)}) async-start(f32[128,1,64]{2,1,0:T(1,128)} %bitcast.5), calls=%async_computation.1 | async-start | bytes 131072 | tf_op jit(solution)/shard_map/all_to_all | solution.py:110
  311.0 55.9 %copy-start.4 = (f32[4,32,32]{2,1,0:T(8,128)S(1)}, f32[4,32,32]{2,1,0:T(8,128)}, u32[]{:S(2)}) copy-start(f32[4,32,32]{2,1,0:T(8,128)} %param.34) | copy-start | bytes 49156
  361.3 5.8 collective-permute-start.19
  364.5 3.1 collective-permute-start.18
  367.7 11.3 %collective-permute-start.21 = (f32[66,1]{1,0:T(8,128)S(1)}, f32[66,1]{1,0:T(8,128)S(1)}, u32[]{:S(2)}, u32[]{:S(2)}) collective-permute-start(f32[66,1]{1,0:T(8,128)S(1)} %get-tuple-element.95), channel_id=1, source_target_pairs={{1,0},{2,1},{3,2},{4,3},{5,4},{6,5},{7,6},{8,7},{9,8},{10,9},{11,1... | collective-permute-start | bytes 800 | tf_op jit(solution)/shard_map/ppermute | solution.py:37
  369.0 10.9 %collective-permute-start.20 = (f32[66,1]{1,0:T(8,128)S(1)}, f32[66,1]{1,0:T(8,128)S(1)}, u32[]{:S(2)}, u32[]{:S(2)}) collective-permute-start(f32[66,1]{1,0:T(8,128)S(1)} %get-tuple-element.94), channel_id=1, source_target_pairs={{0,1},{1,2},{2,3},{3,4},{4,5},{5,6},{6,7},{7,8},{8,9},{9,10},{10,1... | collective-permute-start | bytes 800 | tf_op jit(solution)/shard_map/ppermute | solution.py:34
  380.0 7.1 collective-permute-start.23
  381.9 5.7 collective-permute-start.22
  387.7 6.1 collective-permute-start.25
  389.0 5.6 collective-permute-start.24
  394.8 7.0 collective-permute-start.27
  396.7 5.7 collective-permute-start.26
  402.6 33.3 %collective-permute-start.29 = (f32[66,1]{1,0:T(8,128)S(1)}, f32[66,1]{1,0:T(8,128)S(1)}, u32[]{:S(2)}, u32[]{:S(2)}) collective-permute-start(f32[66,1]{1,0:T(8,128)S(1)} %get-tuple-element.91), channel_id=1, source_target_pairs={{1,0},{2,1},{3,2},{4,3},{5,4},{6,5},{7,6},{8,7},{9,8},{10,9},{11,1... | collective-permute-start | bytes 800 | tf_op jit(solution)/shard_map/ppermute | solution.py:37
  403.8 32.0 %collective-permute-start.28 = (f32[66,1]{1,0:T(8,128)S(1)}, f32[66,1]{1,0:T(8,128)S(1)}, u32[]{:S(2)}, u32[]{:S(2)}) collective-permute-start(f32[66,1]{1,0:T(8,128)S(1)} %get-tuple-element.90), channel_id=1, source_target_pairs={{0,1},{1,2},{2,3},{3,4},{4,5},{5,6},{6,7},{7,8},{8,9},{9,10},{10,1... | collective-permute-start | bytes 800 | tf_op jit(solution)/shard_map/ppermute | solution.py:34
  436.0 62.2 %collective-permute-start.31 = (f32[1,256]{1,0:T(1,128)S(1)}, f32[1,256]{1,0:T(1,128)S(1)}, u32[]{:S(2)}, u32[]{:S(2)}) collective-permute-start(f32[1,256]{1,0:T(1,128)S(1)} %get-tuple-element.113), channel_id=1, source_target_pairs={{16,0},{32,16},{48,32},{64,48},{80,64},{96,80},{112,96},{17,1},{33... | collective-permute-start | bytes 3080 | tf_op jit(solution)/shard_map/ppermute | solution.py:37
  441.2 57.1 %collective-permute-start.30 = (f32[1,256]{1,0:T(1,128)S(1)}, f32[1,256]{1,0:T(1,128)S(1)}, u32[]{:S(2)}, u32[]{:S(2)}) collective-permute-start(f32[1,256]{1,0:T(1,128)S(1)} %get-tuple-element.112), channel_id=1, source_target_pairs={{0,16},{16,32},{32,48},{48,64},{64,80},{80,96},{96,112},{1,17},{17... | collective-permute-start | bytes 3080 | tf_op jit(solution)/shard_map/ppermute | solution.py:34
  494.5 10.2 %all-to-all-start.6 = ((f32[16,256,1]{1,2,0:T(1,128)}), f32[16,256,1]{1,2,0:T(1,128)S(1)}, u32[]{:S(2)}, u32[]{:S(2)}) async-start(f32[16,256,1]{1,2,0:T(1,128)} %concatenate.293), calls=%async_computation.6 | async-start | bytes 32768 | tf_op jit(solution)/shard_map/all_to_all | solution.py:14
  498.4 8.0 collective-permute-start.33
  499.7 6.8 collective-permute-start.32
  552.9 20.6 %all-to-all-start.2 = ((f32[128,1,64]{2,1,0:T(1,128)}), f32[128,1,64]{2,1,0:T(1,128)S(1)}, u32[]{:S(2)}, u32[]{:S(2)}) async-start(f32[128,1,64]{2,1,0:T(1,128)} %bitcast.9), calls=%async_computation.2 | async-start | bytes 131072 | tf_op jit(solution)/shard_map/all_to_all | solution.py:105
  574.1 49.4 %all-to-all-start.4 = ((f32[128,1,64]{2,1,0:T(1,128)}), f32[128,1,64]{2,1,0:T(1,128)S(1)}, u32[]{:S(2)}, u32[]{:S(2)}) async-start(f32[128,1,64]{2,1,0:T(1,128)} %bitcast.24), calls=%async_computation.4 | async-start | bytes 131072 | tf_op jit(solution)/shard_map/all_to_all | solution.py:110
  674.0 5.8 collective-permute-start.35
  677.2 3.1 collective-permute-start.34
  680.3 11.3 %collective-permute-start.37 = (f32[66,1]{1,0:T(8,128)S(1)}, f32[66,1]{1,0:T(8,128)S(1)}, u32[]{:S(2)}, u32[]{:S(2)}) collective-permute-start(f32[66,1]{1,0:T(8,128)S(1)} %get-tuple-element.87), channel_id=1, source_target_pairs={{1,0},{2,1},{3,2},{4,3},{5,4},{6,5},{7,6},{8,7},{9,8},{10,9},{11,1... | collective-permute-start | bytes 800 | tf_op jit(solution)/shard_map/ppermute | solution.py:37
  681.6 10.9 %collective-permute-start.36 = (f32[66,1]{1,0:T(8,128)S(1)}, f32[66,1]{1,0:T(8,128)S(1)}, u32[]{:S(2)}, u32[]{:S(2)}) collective-permute-start(f32[66,1]{1,0:T(8,128)S(1)} %get-tuple-element.86), channel_id=1, source_target_pairs={{0,1},{1,2},{2,3},{3,4},{4,5},{5,6},{6,7},{7,8},{8,9},{9,10},{10,1... | collective-permute-start | bytes 800 | tf_op jit(solution)/shard_map/ppermute | solution.py:34
  692.6 7.1 collective-permute-start.39
  694.6 5.7 collective-permute-start.38
  700.4 6.1 collective-permute-start.41
  701.7 5.6 collective-permute-start.40
  707.5 7.0 collective-permute-start.43
  709.4 5.7 collective-permute-start.42
  715.2 33.3 %collective-permute-start.45 = (f32[66,1]{1,0:T(8,128)S(1)}, f32[66,1]{1,0:T(8,128)S(1)}, u32[]{:S(2)}, u32[]{:S(2)}) collective-permute-start(f32[66,1]{1,0:T(8,128)S(1)} %get-tuple-element.83), channel_id=1, source_target_pairs={{1,0},{2,1},{3,2},{4,3},{5,4},{6,5},{7,6},{8,7},{9,8},{10,9},{11,1... | collective-permute-start | bytes 800 | tf_op jit(solution)/shard_map/ppermute | solution.py:37
  716.5 32.0 %collective-permute-start.44 = (f32[66,1]{1,0:T(8,128)S(1)}, f32[66,1]{1,0:T(8,128)S(1)}, u32[]{:S(2)}, u32[]{:S(2)}) collective-permute-start(f32[66,1]{1,0:T(8,128)S(1)} %get-tuple-element.82), channel_id=1, source_target_pairs={{0,1},{1,2},{2,3},{3,4},{4,5},{5,6},{6,7},{7,8},{8,9},{9,10},{10,1... | collective-permute-start | bytes 800 | tf_op jit(solution)/shard_map/ppermute | solution.py:34
  748.7 62.2 %collective-permute-start.47 = (f32[1,256]{1,0:T(1,128)S(1)}, f32[1,256]{1,0:T(1,128)S(1)}, u32[]{:S(2)}, u32[]{:S(2)}) collective-permute-start(f32[1,256]{1,0:T(1,128)S(1)} %get-tuple-element.105), channel_id=1, source_target_pairs={{16,0},{32,16},{48,32},{64,48},{80,64},{96,80},{112,96},{17,1},{33... | collective-permute-start | bytes 3080 | tf_op jit(solution)/shard_map/ppermute | solution.py:37
  753.9 57.1 %collective-permute-start.46 = (f32[1,256]{1,0:T(1,128)S(1)}, f32[1,256]{1,0:T(1,128)S(1)}, u32[]{:S(2)}, u32[]{:S(2)}) collective-permute-start(f32[1,256]{1,0:T(1,128)S(1)} %get-tuple-element.104), channel_id=1, source_target_pairs={{0,16},{16,32},{32,48},{48,64},{64,80},{80,96},{96,112},{1,17},{17... | collective-permute-start | bytes 3080 | tf_op jit(solution)/shard_map/ppermute | solution.py:34
  807.1 10.2 %all-to-all-start.8 = ((f32[16,256,1]{1,2,0:T(1,128)}), f32[16,256,1]{1,2,0:T(1,128)S(1)}, u32[]{:S(2)}, u32[]{:S(2)}) async-start(f32[16,256,1]{1,2,0:T(1,128)} %concatenate.295), calls=%async_computation.8 | async-start | bytes 32768 | tf_op jit(solution)/shard_map/all_to_all | solution.py:14
  811.0 8.0 collective-permute-start.49
  812.3 6.8 collective-permute-start.48
  865.5 20.6 %all-to-all-start.5 = ((f32[128,1,64]{2,1,0:T(1,128)}), f32[128,1,64]{2,1,0:T(1,128)S(1)}, u32[]{:S(2)}, u32[]{:S(2)}) async-start(f32[128,1,64]{2,1,0:T(1,128)} %bitcast.28), calls=%async_computation.5 | async-start | bytes 131072 | tf_op jit(solution)/shard_map/all_to_all | solution.py:105
  932.4 19.5 %all-to-all-start.7 = ((f32[128,1,64]{2,1,0:T(1,128)}), f32[128,1,64]{2,1,0:T(1,128)S(1)}, u32[]{:S(2)}, u32[]{:S(2)}) async-start(f32[128,1,64]{2,1,0:T(1,128)} %bitcast.37), calls=%async_computation.7 | async-start | bytes 131072 | tf_op jit(solution)/shard_map/all_to_all | solution.py:110
  (8 other events, 21.3 us)
